TPU v7x, 32 devices: a whole 2x2x4 slice. The times are simulated.
32 devices in a mesh: dp: 8 (over z, y), tensor: 4 (over x, core).
Axes of the slice: x: 2, y: 2, z: 4, core: 2. Of those that a mesh axis runs over, the one named last changes fastest.
Arguments:
- tokens: bfloat16 [16384, 768], P(('dp', 'tensor')), may hold values from -6 to 6
- lengths: int32 [8], P('dp'), may hold values from 512 to 2048, as said below
- arrival_slots: int32 [8, 2048], P('dp'), may hold values from 0 to 2047, each once within a row
- w_qkv: float32 [3, 768, 768], P(None, 'dp', 'tensor'), may hold values from -0.21875 to 0.21875
- w_out: float32 [768, 768], P('tensor', 'dp'), may hold values from -1.75 to 1.75
- w_up: float32 [768, 3072], P('dp', 'tensor'), may hold values from -0.21875 to 0.21875
- w_down: float32 [3072, 768], P('tensor', 'dp'), may hold values from -0.109375 to 0.109375
- w_proj: float32 [768, 128], P('dp'), may hold values from -0.21875 to 0.21875
- norm_gains: float32 [2, 768], P(None, 'dp'), may hold values from 0.1 to 1.9
- biases: float32 [6, 768], P(None, 'dp'), may hold values from -4 to 4
- up_bias: float32 [3072], P('dp'), may hold values from -4 to 4
- cotangent: bfloat16 [16384, 128], P(('dp', 'tensor')), may hold values from -6 to 6
Outputs:
- embeddings: float32 [16384, 128], P(('dp', 'tensor'))
- grad_tokens: float32 [16384, 768], P(('dp', 'tensor'))
- grad_qkv: float32 [3, 768, 768], P(None, 'dp', 'tensor')
- grad_out: float32 [768, 768], P('tensor', 'dp')
- grad_up: float32 [768, 3072], P('dp', 'tensor')
- grad_down: float32 [3072, 768], P('tensor', 'dp')
- grad_proj: float32 [768, 128], P('dp')
- grad_gains: float32 [2, 768], P(None, 'dp')
- grad_biases: float32 [6, 768], P(None, 'dp')
- grad_up_bias: float32 [3072], P('dp')
Inputs may be any that keep to these rules, and one draw needn't show every extreme that they name: `lengths`: some passage fills its whole slot of 2048 positions. `arrival_slots`: each row names every slot of its group once.
All inputs are finite; a program needn't handle non-finite values.
Results may differ from a plain program's by a relative error of at most 0.02.
Values may be sent and summed in bfloat16 or wider, within the bound.
A program may use at most 128 MiB of HBM per device.

v0:
```python
import jax
import jax.numpy as jnp
from jax import lax
from jax.sharding import PartitionSpec as P

HEAD_DIM = 64
SLOT = 2048
EPS_NORM = 1e-06
EPS_UNIT = 1e-06
NEG_FILL = -1e30


def norm_rows(values, gain, shift):
    center = values - jnp.mean(values, axis=-1, keepdims=True)
    spread = jnp.mean(center * center, axis=-1, keepdims=True)
    return center * lax.rsqrt(spread + EPS_NORM) * gain + shift


def gelu_exact(values):
    return jax.nn.gelu(values, approximate=False)


def contract_rows(left, right):
    return lax.dot_general(
        left, right, (((0,), (0,)), ((), ())), preferred_element_type=jnp.float32
    )


def times_transposed(left, right):
    return lax.dot_general(
        left, right, (((1,), (1,)), ((), ())), preferred_element_type=jnp.float32
    )


def attend(query_heads, key_heads, value_heads, key_mask, num_blocks, factor):

    def one_block(position):
        passage_idx = position // num_blocks
        block_idx = position % num_blocks
        query_block = query_heads[passage_idx, block_idx]
        scores = (
            jnp.einsum(
                "qhe,khe->hqk",
                query_block,
                key_heads[passage_idx],
                preferred_element_type=jnp.float32,
            )
            * factor
        )
        scores = jnp.where(key_mask[passage_idx][None, None, :], scores, NEG_FILL)
        row_top = jnp.max(scores, axis=-1, keepdims=True)
        shifted = jnp.exp(scores - row_top)
        row_total = jnp.sum(shifted, axis=-1, keepdims=True)
        soft_low = (shifted / row_total).astype(jnp.bfloat16)
        result = jnp.einsum(
            "hqk,khe->qhe", soft_low, value_heads[passage_idx], preferred_element_type=jnp.float32
        )
        return (result, (row_top + jnp.log(row_total))[..., 0])

    return lax.map(one_block, jnp.arange(query_heads.shape[0] * num_blocks))


def attend_back(
    query_heads, key_heads, value_heads, dcontext_heads, log_total, key_mask, num_blocks, factor
):

    def passage(passage_idx):
        key_rows = key_heads[passage_idx]
        value_rows = value_heads[passage_idx]
        mask_row = key_mask[passage_idx][None, None, :]

        def step(carry, block_idx):
            dkey_sum, dvalue_sum = carry
            query_block = query_heads[passage_idx, block_idx]
            dout_block = dcontext_heads[passage_idx, block_idx]
            total_block = log_total[passage_idx * num_blocks + block_idx]
            scores = (
                jnp.einsum(
                    "qhe,khe->hqk", query_block, key_rows, preferred_element_type=jnp.float32
                )
                * factor
            )
            scores = jnp.where(mask_row, scores, NEG_FILL)
            soft_probs = jnp.exp(scores - total_block[..., None])
            dvalue_sum = dvalue_sum + jnp.einsum(
                "hqk,qhe->khe",
                soft_probs.astype(jnp.bfloat16),
                dout_block,
                preferred_element_type=jnp.float32,
            )
            dsoft = jnp.einsum(
                "qhe,khe->hqk", dout_block, value_rows, preferred_element_type=jnp.float32
            )
            dscore = (
                soft_probs * (dsoft - jnp.sum(soft_probs * dsoft, axis=-1, keepdims=True))
            ).astype(jnp.bfloat16)
            dquery = (
                jnp.einsum("hqk,khe->qhe", dscore, key_rows, preferred_element_type=jnp.float32)
                * factor
            )
            dkey_sum = (
                dkey_sum
                + jnp.einsum(
                    "hqk,qhe->khe", dscore, query_block, preferred_element_type=jnp.float32
                )
                * factor
            )
            return ((dkey_sum, dvalue_sum), dquery)

        zero_grad = jnp.zeros(key_rows.shape, jnp.float32)
        (dkey_sum, dvalue_sum), dquery = lax.scan(
            step, (zero_grad, zero_grad), jnp.arange(num_blocks)
        )
        return (dquery, dkey_sum, dvalue_sum)

    return lax.map(passage, jnp.arange(key_heads.shape[0]))


def body(
    tokens,
    lengths,
    arrival_slots,
    w_qkv,
    w_out,
    w_up,
    w_down,
    w_proj,
    norm_gains,
    biases,
    up_bias,
    cotangent,
):
    tensor_size = lax.axis_size("tensor")
    tensor_pos = lax.axis_index("tensor")
    own_rows = tokens.shape[0]
    group_rows = own_rows * tensor_size
    passages = group_rows // SLOT
    block_rows = min(512, SLOT)
    num_blocks = SLOT // block_rows
    factor = HEAD_DIM ** (-0.5)
    slot_order = arrival_slots[0]
    gathered = (
        lax.all_gather(w_qkv.astype(jnp.bfloat16), "dp", axis=1, tiled=True),
        lax.all_gather(w_out.astype(jnp.bfloat16), "dp", axis=1, tiled=True),
        lax.all_gather(w_up.astype(jnp.bfloat16), "dp", axis=0, tiled=True),
        lax.all_gather(w_down.astype(jnp.bfloat16), "dp", axis=1, tiled=True),
        lax.all_gather(w_proj.astype(jnp.bfloat16), "dp", axis=0, tiled=True),
        lax.all_gather(norm_gains.astype(jnp.bfloat16), "dp", axis=1, tiled=True),
        lax.all_gather(biases.astype(jnp.bfloat16), "dp", axis=1, tiled=True),
        lax.all_gather(up_bias.astype(jnp.bfloat16), "dp", axis=0, tiled=True),
    )
    qkv_weight, out_weight, up_weight, down_weight, proj_weight, gain_low, bias_low, upbias_low = (
        gathered
    )
    width_local = qkv_weight.shape[2]
    hidden_local = up_weight.shape[1]
    heads_local = width_local // HEAD_DIM
    gain_full = gain_low.astype(jnp.float32)
    bias_full = bias_low.astype(jnp.float32)
    upbias_full = upbias_low.astype(jnp.float32)
    col_start = tensor_pos * width_local
    query_bias = lax.dynamic_slice_in_dim(bias_full[0], col_start, width_local)
    value_bias = lax.dynamic_slice_in_dim(bias_full[1], col_start, width_local)
    arrived = lax.all_gather(tokens, "tensor", axis=0, tiled=True)
    inverse = (
        jnp.zeros((group_rows,), jnp.int32)
        .at[slot_order]
        .set(jnp.arange(group_rows, dtype=jnp.int32))
    )
    slotted = jnp.take(arrived, inverse, axis=0)
    row_start = tensor_pos * own_rows
    resid_input = lax.dynamic_slice_in_dim(slotted, row_start, own_rows, 0).astype(jnp.float32)
    positions = row_start + jnp.arange(own_rows, dtype=jnp.int32)
    row_keep = (positions % SLOT < lengths[positions // SLOT]).astype(jnp.float32)
    key_mask = jnp.arange(SLOT, dtype=jnp.int32)[None, :] < lengths[:, None]
    qkv_bias = jnp.stack([query_bias, jnp.zeros_like(query_bias), value_bias])
    qkv_all = (
        jnp.einsum("gd,cde->cge", slotted, qkv_weight, preferred_element_type=jnp.float32)
        + qkv_bias[:, None, :]
    ).astype(jnp.bfloat16)
    block_shape = (passages, num_blocks, block_rows, heads_local, HEAD_DIM)
    slot_shape = (passages, SLOT, heads_local, HEAD_DIM)
    query_heads = qkv_all[0].reshape(block_shape)
    key_heads = qkv_all[1].reshape(slot_shape)
    value_heads = qkv_all[2].reshape(slot_shape)
    attended, log_total = attend(query_heads, key_heads, value_heads, key_mask, num_blocks, factor)
    context = attended.reshape(group_rows, width_local).astype(jnp.bfloat16)
    attn_part = lax.psum_scatter(
        jnp.dot(context, out_weight, preferred_element_type=jnp.float32).astype(jnp.bfloat16),
        "tensor",
        scatter_dimension=0,
        tiled=True,
    ).astype(jnp.float32)
    first_sum = resid_input + attn_part + bias_full[2]
    first_norm, back_first = jax.vjp(norm_rows, first_sum, gain_full[0], bias_full[3])
    first_low = first_norm.astype(jnp.bfloat16)
    mid_rows = lax.all_gather(first_low, "tensor", axis=0, tiled=True)
    upbias_own = lax.dynamic_slice_in_dim(upbias_full, tensor_pos * hidden_local, hidden_local)
    ffn_pre = jnp.dot(mid_rows, up_weight, preferred_element_type=jnp.float32) + upbias_own
    hidden = gelu_exact(ffn_pre).astype(jnp.bfloat16)
    ffn_part = lax.psum_scatter(
        jnp.dot(hidden, down_weight, preferred_element_type=jnp.float32).astype(jnp.bfloat16),
        "tensor",
        scatter_dimension=0,
        tiled=True,
    ).astype(jnp.float32)
    second_sum = first_norm + ffn_part + bias_full[4]
    second_norm, back_second = jax.vjp(norm_rows, second_sum, gain_full[1], bias_full[5])
    second_low = second_norm.astype(jnp.bfloat16)
    projected = jnp.dot(second_low, proj_weight, preferred_element_type=jnp.float32)

    def unit_rows(values):
        return (
            values
            * lax.rsqrt(jnp.sum(values * values, axis=-1, keepdims=True) + EPS_UNIT)
            * row_keep[:, None]
        )

    embeddings, back_unit = jax.vjp(unit_rows, projected)
    (dproj,) = back_unit(cotangent.astype(jnp.float32))
    dproj_low = dproj.astype(jnp.bfloat16)
    grad_proj = contract_rows(second_low, dproj_low)
    dsecond_norm = times_transposed(dproj_low, proj_weight)
    dsecond, grad_gain_two, grad_shift_two = back_second(dsecond_norm)
    dsecond_low = dsecond.astype(jnp.bfloat16)
    dsecond_rows = lax.all_gather(dsecond_low, "tensor", axis=0, tiled=True)
    dhidden = times_transposed(dsecond_rows, down_weight)
    grad_down = contract_rows(hidden, dsecond_rows)
    (dpre,) = jax.vjp(gelu_exact, ffn_pre)[1](dhidden)
    dpre_low = dpre.astype(jnp.bfloat16)
    grad_upbias = lax.dynamic_update_slice_in_dim(
        jnp.zeros(upbias_full.shape, jnp.float32),
        jnp.sum(dpre_low.astype(jnp.float32), axis=0),
        tensor_pos * hidden_local,
        0,
    )
    grad_up = contract_rows(mid_rows, dpre_low)
    dfirst_norm = lax.psum_scatter(
        times_transposed(dpre_low, up_weight).astype(jnp.bfloat16),
        "tensor",
        scatter_dimension=0,
        tiled=True,
    ).astype(jnp.float32)
    dfirst, grad_gain_one, grad_shift_one = back_first(dfirst_norm + dsecond)
    dfirst_low = dfirst.astype(jnp.bfloat16)
    dfirst_rows = lax.all_gather(dfirst_low, "tensor", axis=0, tiled=True)
    dcontext = times_transposed(dfirst_rows, out_weight).astype(jnp.bfloat16)
    grad_out = contract_rows(context, dfirst_rows)
    dquery, dkey, dvalue = attend_back(
        query_heads,
        key_heads,
        value_heads,
        dcontext.reshape(block_shape),
        log_total,
        key_mask,
        num_blocks,
        factor,
    )
    dqkv = jnp.stack(
        [
            dquery.reshape(group_rows, width_local),
            dkey.reshape(group_rows, width_local),
            dvalue.reshape(group_rows, width_local),
        ]
    ).astype(jnp.bfloat16)
    grad_qkv = jnp.einsum("gd,cge->cde", slotted, dqkv, preferred_element_type=jnp.float32)
    column_sums = jnp.sum(dqkv.astype(jnp.float32), axis=1)
    resid_full = lax.dynamic_update_slice_in_dim(
        jnp.zeros((group_rows, dfirst.shape[1]), jnp.float32), dfirst, row_start, 0
    )
    chosen = jnp.take(dqkv, slot_order, axis=1)
    through = jnp.einsum("cge,cde->gd", chosen, qkv_weight, preferred_element_type=jnp.float32)
    grad_tokens = lax.psum_scatter(
        (through + jnp.take(resid_full, slot_order, axis=0)).astype(jnp.bfloat16),
        "tensor",
        scatter_dimension=0,
        tiled=True,
    ).astype(jnp.float32)
    zero_row = jnp.zeros((bias_full.shape[1],), jnp.float32)
    grad_biases = jnp.stack(
        [
            lax.dynamic_update_slice_in_dim(zero_row, column_sums[0], col_start, 0),
            lax.dynamic_update_slice_in_dim(zero_row, column_sums[2], col_start, 0),
            jnp.sum(dfirst, axis=0),
            grad_shift_one,
            jnp.sum(dsecond, axis=0),
            grad_shift_two,
        ]
    )
    grad_gains = jnp.stack([grad_gain_one, grad_gain_two])
    grad_proj, grad_gains, grad_biases, grad_upbias = (
        lax.psum(grad_proj.astype(jnp.bfloat16), "tensor").astype(jnp.float32),
        lax.psum(grad_gains.astype(jnp.bfloat16), "tensor").astype(jnp.float32),
        lax.psum(grad_biases.astype(jnp.bfloat16), "tensor").astype(jnp.float32),
        lax.psum(grad_upbias.astype(jnp.bfloat16), "tensor").astype(jnp.float32),
    )
    summed = (
        lax.psum_scatter(grad_qkv, "dp", scatter_dimension=1, tiled=True),
        lax.psum_scatter(grad_out, "dp", scatter_dimension=1, tiled=True),
        lax.psum_scatter(grad_up, "dp", scatter_dimension=0, tiled=True),
        lax.psum_scatter(grad_down, "dp", scatter_dimension=1, tiled=True),
        lax.psum_scatter(grad_proj, "dp", scatter_dimension=0, tiled=True),
        lax.psum_scatter(grad_gains, "dp", scatter_dimension=1, tiled=True),
        lax.psum_scatter(grad_biases, "dp", scatter_dimension=1, tiled=True),
        lax.psum_scatter(grad_upbias, "dp", scatter_dimension=0, tiled=True),
    )
    return (
        embeddings,
        grad_tokens,
        summed[0],
        summed[1],
        summed[2],
        summed[3],
        summed[4],
        summed[5],
        summed[6],
        summed[7],
    )


def solution(mesh):
    return jax.shard_map(
        body,
        mesh=mesh,
        in_specs=(
            P(("dp", "tensor"), None),
            P("dp"),
            P("dp", None),
            P(None, "dp", "tensor"),
            P("tensor", "dp"),
            P("dp", "tensor"),
            P("tensor", "dp"),
            P("dp", None),
            P(None, "dp"),
            P(None, "dp"),
            P("dp"),
            P(("dp", "tensor"), None),
        ),
        out_specs=(
            P(("dp", "tensor"), None),
            P(("dp", "tensor"), None),
            P(None, "dp", "tensor"),
            P("tensor", "dp"),
            P("dp", "tensor"),
            P("tensor", "dp"),
            P("dp", None),
            P(None, "dp"),
            P(None, "dp"),
            P("dp"),
        ),
        check_vma=False,
    )
```

profile of v0, /device:TPU:0, one launch (start us, length us, event | category | flops | bytes accessed | tf_op | source)
XLA Modules:
  0.0 1148.0 jit_solution(114364910664673060)
XLA Ops:
  9.5 27.9 %all-gather = bf16[8,96,6]{1,2,0:T(8,128)(2,1)S(1)} all-gather(bf16[1,96,6]{1,2,0:T(8,128)(2,1)S(1)} %convert_bitcast_fusion), channel_id=1, replica_groups=mesh['dp'=8,'tensor'=4] {'dp'}, dimensions={0}, use_global_device_ids=true | all-gather | bytes 10368 | tf_op jit(solution)/shard_map/all_gather | solution.py:149
  39.6 36.3 %all_gather.37 = bf16[3,768,192]{2,0,1:T(4,128)(2,1)S(1)} all-gather(bf16[3,96,192]{2,0,1:T(4,128)(2,1)S(1)} %copy.61), channel_id=1, replica_groups=mesh['dp'=8,'tensor'=4] {'dp'}, dimensions={1}, use_global_device_ids=true | all-gather | bytes 995328 | tf_op jit(solution)/shard_map/all_gather | solution.py:143
  77.0 8.0 scatter_custom_fusion
  85.7 31.1 %all_gather.39 = bf16[192,768]{0,1:T(8,128)(2,1)S(1)} all-gather(bf16[192,96]{0,1:T(8,128)(2,1)S(1)} %copy.66), channel_id=1, replica_groups=mesh['dp'=8,'tensor'=4] {'dp'}, dimensions={1}, use_global_device_ids=true | all-gather | bytes 331776 | tf_op jit(solution)/shard_map/all_gather | solution.py:144
  117.0 12.4 %gather_fusion = bf16[2048,768]{1,0:T(8,128)(2,1)} fusion(bf16[2048,768]{1,0:T(8,128)(2,1)} %all-gather.10.cloned.1.call-done, s32[2048]{0:T(1024)S(1)} %fusion.65), kind=kCustom, calls=%fused_computation | custom fusion | bytes 6299648 | tf_op jit(solution)/shard_map/jit(_take)/gather | solution.py:170
  134.9 49.4 %while.44 = (s32[]{:T(128)}, bf16[4,512,3,64]{1,3,2,0:T(8,128)(2,1)S(1)}, f32[4,3,512]{2,1,0:T(4,128)}, s32[4]{0:T(128)S(1)}, bf16[1,4,512,3,64]{2,4,3,1,0:T(8,1...) while((s32[]{:T(128)}, ...), condition=%wide.region_4.5_spmd.clone, body=%wide.region_1.4_spmd.clone.sunk | while | flops 843055616 | bytes 39975208 | solution.py:60
  189.5 18.1 %all-gather.1 = bf16[8,96,2]{1,2,0:T(2,128)(2,1)S(1)} all-gather(bf16[1,96,2]{1,2,0:T(2,128)(2,1)S(1)} %convert_bitcast_fusion.1), channel_id=1, replica_groups=mesh['dp'=8,'tensor'=4] {'dp'}, dimensions={0}, use_global_device_ids=true | all-gather | bytes 3456 | tf_op jit(solution)/shard_map/all_gather | solution.py:148
  207.7 16.3 %reduce-scatter.20.cloned.1.call-done = bf16[512,768]{1,0:T(8,128)(2,1)} async-done(((bf16[2048,768]{1,0:T(8,128)(2,1)}), bf16[512,768]{1,0:T(8,128)(2,1)}) %reduce-scatter.20.cloned.1.call-update) | async-done | bytes 786448 | tf_op jit(solution)/shard_map/reduce_scatter | solution.py:188
  231.1 26.3 %all-gather.2 = bf16[8,1,384]{2,1,0:T(2,128)(2,1)S(1)} all-gather(bf16[1,1,384]{2,1,0:T(2,128)(2,1)S(1)} %reshape.272), channel_id=1, replica_groups=mesh['dp'=8,'tensor'=4] {'dp'}, dimensions={0}, use_global_device_ids=true | all-gather | bytes 6912 | tf_op jit(solution)/shard_map/all_gather | solution.py:150
  259.3 19.0 %multiply_convert_fusion.1 = (bf16[2048,768]{1,0:T(8,128)(2,1)}, f32[2048,768]{1,0:T(8,128)}, f32[2048,768]{1,0:T(8,128)}) fusion(f32[768]{0:T(1024)S(1)} %dynamic_slice.71, bf16[2048,768]{1,0:T(8,128)(2,1)} %all-gather.12.cloned.1.call-done, bf16[768,768]{1,0:T(8,128)(2,1)} %all-gather.14.cloned.1.call-done), kind=kOutput, calls=%fused_computation.62 | convolution fusion | flops 2519728128 | bytes 20057088 | tf_op jit(solution)/shard_map/dot_general | solution.py:199
  278.3 25.1 %all-gather.16.cloned.1.call-done = bf16[768,768]{0,1:T(8,128)(2,1)} async-done(((bf16[768,96]{0,1:T(8,128)(2,1)}), bf16[768,768]{0,1:T(8,128)(2,1)}) %all-gather.16.cloned.1.call-update) | async-done | bytes 1179664 | tf_op jit(solution)/shard_map/all_gather | solution.py:146
  303.4 6.6 convolution_convert_fusion.1
  311.0 30.6 %all_gather.45 = bf16[768,128]{1,0:T(8,128)(2,1)S(1)} all-gather(bf16[96,128]{1,0:T(8,128)(2,1)S(1)} %convert_element_type.175), channel_id=1, replica_groups=mesh['dp'=8,'tensor'=4] {'dp'}, dimensions={0}, use_global_device_ids=true | all-gather | bytes 221184 | tf_op jit(solution)/shard_map/all_gather | solution.py:147
  354.9 28.2 %all-gather.18.cloned.1.call-done = bf16[2048,768]{1,0:T(8,128)(2,1)} async-done(((bf16[512,768]{1,0:T(8,128)(2,1)}), bf16[2048,768]{1,0:T(8,128)(2,1)}) %all-gather.18.cloned.1.call-update) | async-done | bytes 3145744 | tf_op jit(solution)/shard_map/all_gather | solution.py:226
  383.1 11.1 convert_reduce_fusion
  400.0 37.8 %reduce-scatter.24.cloned.1.call-done = bf16[512,768]{1,0:T(8,128)(2,1)} async-done(((bf16[2048,768]{1,0:T(8,128)(2,1)}), bf16[512,768]{1,0:T(8,128)(2,1)}) %reduce-scatter.24.cloned.1.call-update) | async-done | bytes 786448 | tf_op jit(solution)/shard_map/reduce_scatter | solution.py:238
  457.9 19.7 %all-gather.20.cloned.1.call-done = bf16[2048,768]{1,0:T(8,128)(2,1)} async-done(((bf16[512,768]{1,0:T(8,128)(2,1)}), bf16[2048,768]{1,0:T(8,128)(2,1)}) %all-gather.20.cloned.1.call-update) | async-done | bytes 3145744 | tf_op jit(solution)/shard_map/all_gather | solution.py:246
  487.7 119.7 %while.45 = (s32[]{:T(128)}, f32[2048,3,64]{0,2,1:T(8,128)S(1)}, f32[2048,3,64]{0,2,1:T(8,128)}, bf16[4,512,3,64]{1,3,2,0:T(8,128)(2,1)}, s32[4]{0:T(128)S(1)}, ...) while((s32[]{:T(128)}, f32[2048,3,64]{0,2,1:T(8,128)S(1)}, ...), condition=%wide.region_20.21_spmd.clone, body=%wide.region_18.20_spmd.clone.sunk | while | flops 2062516736 | bytes 129419512 | solution.py:111
  494.4 4.9 fusion.148
  499.3 4.8 multiply_reduce_fusion.10
  504.2 5.0 multiply_convert_fusion.3
  509.1 5.7 fusion.149
  523.8 5.5 fusion.148
  529.3 4.8 multiply_reduce_fusion.10
  534.2 5.0 multiply_convert_fusion.3
  539.2 5.6 fusion.149
  553.8 5.5 fusion.148
  564.2 5.0 multiply_convert_fusion.3
  569.2 5.6 fusion.149
  583.9 5.5 fusion.148
  589.4 4.8 multiply_reduce_fusion.10
  594.3 5.0 multiply_convert_fusion.3
  599.2 5.6 fusion.149
  613.8 10.6 all-reduce.1
  642.9 13.4 %gather_fusion.2 = f32[2048,768]{1,0:T(8,128)} fusion(f32[2048,768]{1,0:T(8,128)} %get-tuple-element.574, s32[2048]{0:T(1024)S(1)} %broadcast_clamp_fusion), kind=kCustom, calls=%fused_computation.2 | custom fusion | bytes 12591104 | tf_op jit(solution)/shard_map/jit(_take)/gather | solution.py:274
  656.4 7.0 copy.72
  663.3 18.9 %gather_fusion.1 = bf16[2048,3,192]{2,1,0:T(4,128)(2,1)} fusion(bf16[3,2048,192]{2,0,1:T(4,128)(2,1)} %copy.72, s32[2048]{0:T(1024)S(1)} %broadcast_clamp_fusion), kind=kCustom, calls=%fused_computation.1 | custom fusion | bytes 4726784 | tf_op jit(solution)/shard_map/jit(_take)/gather | solution.py:271
  682.2 9.7 select_bitcast_fusion
  691.9 6.2 fusion.48
  700.3 7.0 fusion.81
  707.3 6.9 fusion.82
  716.4 37.2 %all-reduce = f32[3072]{0:T(1024)S(1)} all-reduce(bf16[3072]{0:T(1024)(128)(2,1)S(1)} %get-tuple-element.552), channel_id=13, replica_groups=mesh['dp'=8,'tensor'=4] {'dp'}, use_global_device_ids=true, to_apply=%region_41.42.clone | all-reduce | flops 3072 | bytes 18432
  757.2 62.2 %reduce-scatter.36.cloned.1.call-done = f32[96,192]{1,0:T(8,128)} async-done(((f32[768,192]{1,0:T(8,128)}), f32[96,192]{1,0:T(8,128)}) %reduce-scatter.36.cloned.1.call-update) | async-done | bytes 73744
  821.0 67.9 %reduce-scatter.34.cloned.1.call-done = f32[96,576]{1,0:T(8,128)} async-done(((f32[768,576]{1,0:T(8,128)}), f32[96,576]{1,0:T(8,128)}) %reduce-scatter.34.cloned.1.call-update) | async-done | bytes 221200
  890.8 37.6 %reduce-scatter.26.cloned.1.call-done = bf16[512,768]{1,0:T(8,128)(2,1)} async-done(((bf16[2048,768]{1,0:T(8,128)(2,1)}), bf16[512,768]{1,0:T(8,128)(2,1)}) %reduce-scatter.26.cloned.1.call-update) | async-done | bytes 786448 | tf_op jit(solution)/shard_map/reduce_scatter | solution.py:273
  930.8 63.5 %reduce-scatter.32.cloned.1.call-done = f32[96,128]{1,0:T(8,128)} async-done(((f32[768,128]{1,0:T(8,128)}), f32[96,128]{1,0:T(8,128)}) %reduce-scatter.32.cloned.1.call-update) | async-done | bytes 49168 | tf_op jit(solution)/shard_map/reduce_scatter | solution.py:302
  994.4 72.9 %reduce-scatter.28.cloned.1.call-done = f32[96,768]{1,0:T(8,128)} async-done(((f32[768,768]{1,0:T(8,128)}), f32[96,768]{1,0:T(8,128)}) %reduce-scatter.28.cloned.1.call-update) | async-done | bytes 294928 | tf_op jit(solution)/shard_map/reduce_scatter | solution.py:300
  1067.3 73.1 %reduce-scatter.30.cloned.1.call-done = f32[768,96]{0,1:T(8,128)} async-done(((f32[768,768]{0,1:T(8,128)}), f32[768,96]{0,1:T(8,128)}) %reduce-scatter.30.cloned.1.call-update) | async-done | bytes 294928 | tf_op jit(solution)/shard_map/reduce_scatter | solution.py:301
  (289 shorter events, 186.6 us)
Async XLA Ops:
  8.0 68.9 %copy-start.19 = (s32[1,2048]{1,0:T(1,128)S(1)}, s32[1,2048]{1,0:T(1,128)}, u32[]{:S(2)}) copy-start(s32[1,2048]{1,0:T(1,128)} %param.18) | copy-start | bytes 24580
  8.0 109.0 %all-gather.10.cloned.1.call-start = ((), (), s32[]{:S(2)}) async-start(), calls=%async_computation.11 | async-start | bytes 3932160 | tf_op jit(solution)/shard_map/all_gather | solution.py:164
  8.8 215.3 %reduce-scatter.20.cloned.1.call-start = ((), (), s32[]{:S(2)}) async-start(), calls=%async_computation.12 | async-start | bytes 3932160 | tf_op jit(solution)/shard_map/reduce_scatter | solution.py:188
  76.8 54.7 %copy-start.12 = (bf16[3,768,192]{1,2,0:T(8,128)(2,1)}, bf16[3,768,192]{1,2,0:T(8,128)(2,1)S(1)}, u32[]{:S(2)}) copy-start(bf16[3,768,192]{1,2,0:T(8,128)(2,1)S(1)} %copy.62) | copy-start | bytes 2654212
  76.9 52.4 %copy-start.21 = (s32[2048,1]{0,1:T(1,128)}, s32[2048,1]{0,1:T(1,128)S(1)}, u32[]{:S(2)}) copy-start(s32[2048,1]{0,1:T(1,128)S(1)} %compare_select_fusion) | copy-start | bytes 24580
  185.1 4.4 copy-start.39
  187.8 69.7 %all-gather.14.cloned.1.call-start = ((), (), s32[]{:S(2)}) async-start(), calls=%async_computation.14 | async-start | bytes 1327104 | tf_op jit(solution)/shard_map/all_gather | solution.py:145
  189.4 69.9 %all-gather.12.cloned.1.call-start = ((), (), s32[]{:S(2)}) async-start(), calls=%async_computation.13 | async-start | bytes 3932160 | tf_op jit(solution)/shard_map/all_gather | solution.py:197
  224.0 6.2 copy-start.15
  224.0 7.0 copy-start.37
  230.2 73.2 %all-gather.16.cloned.1.call-start = ((), (), s32[]{:S(2)}) async-start(), calls=%async_computation.15 | async-start | bytes 1327104 | tf_op jit(solution)/shard_map/all_gather | solution.py:146
  231.0 115.2 %reduce-scatter.22.cloned.1.call-start = ((), (), s32[]{:S(2)}) async-start(), calls=%async_computation.16 | async-start | bytes 3932160 | tf_op jit(solution)/shard_map/reduce_scatter | solution.py:201
  257.5 20.9 %copy-start.35 = (f32[768]{0:T(1024)}, f32[768]{0:T(1024)S(1)}, u32[]{:S(2)}) copy-start(f32[768]{0:T(1024)S(1)} %dynamic_slice.71) | copy-start | bytes 9220
  310.0 36.2 %copy-start.18 = (f32[768]{0:T(1024)S(1)}, f32[768]{0:T(1024)}, u32[]{:S(2)}) copy-start(f32[768]{0:T(1024)} %get-tuple-element.508) | copy-start | bytes 9220
  310.0 36.2 %copy-start.28 = (f32[768]{0:T(1024)S(1)}, f32[768]{0:T(1024)}, u32[]{:S(2)}) copy-start(f32[768]{0:T(1024)} %get-tuple-element.507) | copy-start | bytes 9220
  310.0 38.7 %copy-start.27 = (f32[768]{0:T(1024)S(1)}, f32[768]{0:T(1024)}, u32[]{:S(2)}) copy-start(f32[768]{0:T(1024)} %get-tuple-element.506) | copy-start | bytes 9220
  310.0 73.1 %all-gather.18.cloned.1.call-start = ((), (), s32[]{:S(2)}) async-start(), calls=%async_computation.17 | async-start | bytes 3932160 | tf_op jit(solution)/shard_map/all_gather | solution.py:226
  351.6 31.6 %copy-start.36 = (f32[768]{0:T(1024)S(1)}, f32[768]{0:T(1024)}, u32[]{:S(2)}) copy-start(f32[768]{0:T(1024)} %copy-done.35) | copy-start | bytes 9220
  352.2 42.0 %copy-start.23 = (f32[512]{0:T(512)}, f32[512]{0:T(512)S(1)}, u32[]{:S(2)}) copy-start(f32[512]{0:T(512)S(1)} %negate_multiply_fusion.2) | copy-start | bytes 6148
  354.5 83.3 %reduce-scatter.24.cloned.1.call-start = ((), (), s32[]{:S(2)}) async-start(), calls=%async_computation.18 | async-start | bytes 3932160 | tf_op jit(solution)/shard_map/reduce_scatter | solution.py:238
  383.1 12.8 %copy-start.38 = (bf16[768,768]{1,0:T(8,128)(2,1)S(1)}, bf16[768,768]{1,0:T(8,128)(2,1)}, u32[]{:S(2)}) copy-start(bf16[768,768]{1,0:T(8,128)(2,1)} %all-gather.14.cloned.1.call-done) | copy-start | bytes 3538948
  399.9 77.7 %all-gather.20.cloned.1.call-start = ((), (), s32[]{:S(2)}) async-start(), calls=%async_computation.19 | async-start | bytes 3932160 | tf_op jit(solution)/shard_map/all_gather | solution.py:246
  437.8 4.3 copy-start.3
  437.8 4.3 copy-start.9
  448.9 249.3 %all-reduce.4.cloned.1.call-start = ((), (), s32[]{:S(2)}) async-start(), calls=%async_computation.23 | async-start | bytes 393216 | tf_op jit(solution)/shard_map/psum | solution.py:292
  452.5 301.7 %reduce-scatter.38.cloned.1.call-start = ((), (), s32[]{:S(2)}) async-start(), calls=%async_computation.27 | async-start | bytes 442368
  453.6 33.1 %copy-start.24 = (bf16[3072]{0:T(1024)(128)(2,1)}, bf16[3072]{0:T(1024)(128)(2,1)S(1)}, u32[]{:S(2)}) copy-start(bf16[3072]{0:T(1024)(128)(2,1)S(1)} %dynamic_update_slice.46) | copy-start | bytes 18436
  509.1 5.7 copy-start
  539.2 5.6 copy-start
  569.2 5.6 copy-start
  599.2 5.6 copy-start
  609.9 3.8 copy-start.30
  609.9 3.8 copy-start.31
  609.9 3.8 copy-start.25
  609.9 3.8 copy-start.29
  611.4 14.9 %copy-start.8 = (bf16[24,8,4,512]{3,1,2,0:T(8,128)(2,1)S(1)}, bf16[24,8,4,512]{3,1,2,0:T(8,128)(2,1)}, u32[]{:S(2)}) copy-start(bf16[24,8,4,512]{3,1,2,0:T(8,128)(2,1)} %copy-done.7) | copy-start | bytes 2359300
  625.3 130.4 %reduce-scatter.40.cloned.1.call-start = ((), (), s32[]{:S(2)}) async-start(), calls=%async_computation.28 | async-start | bytes 442368
  626.3 193.1 %reduce-scatter.36.cloned.1.call-start = ((), (), s32[]{:S(2)}) async-start(), calls=%async_computation.26 | async-start | bytes 884736
  630.5 258.4 %reduce-scatter.34.cloned.1.call-start = ((), (), s32[]{:S(2)}) async-start(), calls=%async_computation.25 | async-start | bytes 2211840
  638.1 4.8 copy-start.20
  638.1 4.8 copy-start.22
  642.8 285.6 %reduce-scatter.26.cloned.1.call-start = ((), (), s32[]{:S(2)}) async-start(), calls=%async_computation.20 | async-start | bytes 3932160 | tf_op jit(solution)/shard_map/reduce_scatter | solution.py:273
  682.2 9.7 copy-start.13
  698.2 296.2 %reduce-scatter.32.cloned.1.call-start = ((), (), s32[]{:S(2)}) async-start(), calls=%async_computation.24 | async-start | bytes 442368 | tf_op jit(solution)/shard_map/reduce_scatter | solution.py:302
  700.0 367.3 %reduce-scatter.28.cloned.1.call-start = ((), (), s32[]{:S(2)}) async-start(), calls=%async_computation.21 | async-start | bytes 2654208 | tf_op jit(solution)/shard_map/reduce_scatter | solution.py:300
  707.3 7.1 copy-start.40
  707.3 8.3 copy-start.11
  707.3 433.1 %reduce-scatter.30.cloned.1.call-start = ((), (), s32[]{:S(2)}) async-start(), calls=%async_computation.22 | async-start | bytes 2654208 | tf_op jit(solution)/shard_map/reduce_scatter | solution.py:301
  (15 other events, 35.3 us)
Sparse Core Ops, SparseCore 0:
  10.4 31.2 all-gather.9
  187.9 36.0 reduce-scatter.19
  354.6 28.5 all-gather.17
  449.0 28.4 all-gather.19
  480.3 31.9 all-reduce.3
Sparse Core Ops, SparseCore 1:
  191.0 39.5 all-gather.13
  232.6 26.7 all-gather.11
  262.0 41.4 all-gather.15
  310.1 36.0 reduce-scatter.21
  400.0 37.7 reduce-scatter.23
  625.4 63.2 reduce-scatter.37
  691.8 61.3 reduce-scatter.39
  756.9 62.4 reduce-scatter.35
  822.7 66.2 reduce-scatter.33
  891.5 36.9 reduce-scatter.25
  932.2 62.1 reduce-scatter.31
  998.5 68.8 reduce-scatter.27
  1071.2 69.1 reduce-scatter.29
where the time goes:
time: 1150 us
  waiting for transfers between devices  512 us (45%)
  blocking collectives  218 us (19%)
  matrix products  189 us (16%)
  local copies, waits for them, and re-layouts  112 us (10%)
  other arithmetic  81.9 us (7%)
  between operations  18 us (2%)
  loops' own time  16 us (1%)
    unnamed x22, waiting for transfers between devices  131 us
    reduce_scatter x1, waiting for transfers between devices, body(): lax.psum_scatter(grad_down, 'dp', scatter_dimension=1, tiled=True)  73.1 us
    reduce_scatter x1, waiting for transfers between devices, body(): lax.psum_scatter(grad_up, 'dp', scatter_dimension=0, tiled=True)  72.9 us
    reduce_scatter x1, waiting for transfers between devices, body(): lax.psum_scatter(grad_proj, 'dp', scatter_dimension=0, tiled=True)  63.5 us
    reduce_scatter x1, waiting for transfers between devices, body(): lax.psum_scatter(times_transposed(dpre_low, up_weight).astype(jnp.bfloat1...  37.8 us
    reduce_scatter x1, waiting for transfers between devices, body(): lax.psum_scatter((through + jnp.take(resid_full, slot_order, axis=0)).ast...  37.6 us
    unnamed x1, blocking collectives  37.2 us
    all_gather x1, blocking collectives, body(): lax.all_gather(w_qkv.astype(jnp.bfloat16), 'dp', axis=1, tiled=True)  36.3 us
  transfers between devices with their start and end apart: 18, of which 13 were waited for; matrix products, arithmetic and copies ran while one was open for 24% of the time, Pallas kernels for 0%

commit v1 on v0

--- a/solution.py
+++ b/solution.py
@@ -223,7 +223,16 @@
     dsecond_norm = times_transposed(dproj_low, proj_weight)
     dsecond, grad_gain_two, grad_shift_two = back_second(dsecond_norm)
     dsecond_low = dsecond.astype(jnp.bfloat16)
-    dsecond_rows = lax.all_gather(dsecond_low, "tensor", axis=0, tiled=True)
+    far_arr = lax.axis_size("tensor")
+    arr_next = lax.axis_index("tensor")
+    passed, a_next, h_now = (far_arr, arr_next, dsecond_low.shape[0])
+    met_up, answer = (dsecond_low, 1)
+    while answer < passed:
+        g_now = tuple(((nth, (nth - answer) % passed) for nth in range(passed)))
+        mid_arr = lax.ppermute(met_up, "tensor", g_now)
+        met_up = jnp.concatenate([met_up, mid_arr], axis=0)
+        answer = 2 * answer
+    dsecond_rows = jnp.roll(met_up, a_next * h_now, axis=0)
     dhidden = times_transposed(dsecond_rows, down_weight)
     grad_down = contract_rows(hidden, dsecond_rows)
     (dpre,) = jax.vjp(gelu_exact, ffn_pre)[1](dhidden)

time: 1150 us -> 1180 us (1.026)
  waiting for transfers between devices: 512 us -> 529 us
    ppermute x0 -> x2, waiting for transfers between devices: none -> 44.4 us  [body(): mid_arr = lax.ppermute(met_up, 'tensor', g_now)]
    all_gather x1 -> x0, waiting for transfers between devices: 28.2 us -> none  [body(): dsecond_rows = lax.all_gather(dsecond_low, 'tensor', axis=0, tiled=True)]
    unnamed x100 -> x110, local copies, waits for them, and re-layouts: 25.4 us -> 29.7 us
    unnamed x22 -> x21, waiting for transfers between devices: 131 us -> 131 us
  transfers between devices with their start and end apart: 18 -> 19, of which waited for: 13 -> 14; matrix products, arithmetic and copies ran while one was open for 24% -> 24% of each run, Pallas kernels for 0% -> 0%
where the time goes in v1:
time: 1180 us; the launch traced here: 1170 us
  waiting for transfers between devices  529 us (45%)
  blocking collectives  218 us (18%)
  matrix products  188 us (16%)
  local copies, waits for them, and re-layouts  119 us (10%)
  other arithmetic  83.4 us (7%)
  between operations  18 us (2%)
  loops' own time  16 us (1%)
    unnamed x21, waiting for transfers between devices  131 us
    reduce_scatter x1, waiting for transfers between devices, body(): lax.psum_scatter(grad_up, 'dp', scatter_dimension=0, tiled=True)  73.3 us
    reduce_scatter x1, waiting for transfers between devices, body(): lax.psum_scatter(grad_down, 'dp', scatter_dimension=1, tiled=True)  72.9 us
    reduce_scatter x1, waiting for transfers between devices, body(): lax.psum_scatter(grad_proj, 'dp', scatter_dimension=0, tiled=True)  63.5 us
    ppermute x2, waiting for transfers between devices, body(): mid_arr = lax.ppermute(met_up, 'tensor', g_now)  44.4 us
    reduce_scatter x1, waiting for transfers between devices, body(): lax.psum_scatter(times_transposed(dpre_low, up_weight).astype(jnp.bfloat1...  39.1 us
    reduce_scatter x1, waiting for transfers between devices, body(): lax.psum_scatter((through + jnp.take(resid_full, slot_order, axis=0)).ast...  37.3 us
    unnamed x1, blocking collectives  37.3 us
  transfers between devices with their start and end apart: 19, of which 14 were waited for; matrix products, arithmetic and copies ran while one was open for 24% of the time, Pallas kernels for 0%

profile of v1, /device:TPU:0, one launch (start us, length us, event | category | flops | bytes accessed | tf_op | source)
XLA Modules:
  0.0 1174.4 jit_solution(6358301920727628544)
XLA Ops:
  9.5 27.9 %all-gather = bf16[8,96,6]{1,2,0:T(8,128)(2,1)S(1)} all-gather(bf16[1,96,6]{1,2,0:T(8,128)(2,1)S(1)} %convert_bitcast_fusion), channel_id=1, replica_groups=mesh['dp'=8,'tensor'=4] {'dp'}, dimensions={0}, use_global_device_ids=true | all-gather | bytes 10368 | tf_op jit(solution)/shard_map/all_gather | solution.py:149
  39.6 36.3 %all_gather.34 = bf16[3,768,192]{2,0,1:T(4,128)(2,1)S(1)} all-gather(bf16[3,96,192]{2,0,1:T(4,128)(2,1)S(1)} %copy.61), channel_id=1, replica_groups=mesh['dp'=8,'tensor'=4] {'dp'}, dimensions={1}, use_global_device_ids=true | all-gather | bytes 995328 | tf_op jit(solution)/shard_map/all_gather | solution.py:143
  77.0 8.0 scatter_custom_fusion
  85.7 31.2 %all_gather.36 = bf16[192,768]{0,1:T(8,128)(2,1)S(1)} all-gather(bf16[192,96]{0,1:T(8,128)(2,1)S(1)} %copy.66), channel_id=1, replica_groups=mesh['dp'=8,'tensor'=4] {'dp'}, dimensions={1}, use_global_device_ids=true | all-gather | bytes 331776 | tf_op jit(solution)/shard_map/all_gather | solution.py:144
  117.1 12.4 %gather_fusion = bf16[2048,768]{1,0:T(8,128)(2,1)} fusion(bf16[2048,768]{1,0:T(8,128)(2,1)} %all-gather.9.cloned.1.call-done, s32[2048]{0:T(1024)S(1)} %fusion.71), kind=kCustom, calls=%fused_computation | custom fusion | bytes 6299648 | tf_op jit(solution)/shard_map/jit(_take)/gather | solution.py:170
  135.0 49.4 %while.44 = (s32[]{:T(128)}, bf16[4,512,3,64]{1,3,2,0:T(8,128)(2,1)S(1)}, f32[4,3,512]{2,1,0:T(4,128)}, s32[4]{0:T(128)S(1)}, bf16[1,4,512,3,64]{2,4,3,1,0:T(8,1...) while((s32[]{:T(128)}, ...), condition=%wide.region_4.5_spmd.clone, body=%wide.region_1.4_spmd.clone.sunk | while | flops 843055616 | bytes 39975208 | solution.py:60
  189.6 18.1 %all-gather.1 = bf16[8,96,2]{1,2,0:T(2,128)(2,1)S(1)} all-gather(bf16[1,96,2]{1,2,0:T(2,128)(2,1)S(1)} %convert_bitcast_fusion.1), channel_id=1, replica_groups=mesh['dp'=8,'tensor'=4] {'dp'}, dimensions={0}, use_global_device_ids=true | all-gather | bytes 3456 | tf_op jit(solution)/shard_map/all_gather | solution.py:148
  207.8 16.2 %reduce-scatter.20.cloned.1.call-done = bf16[512,768]{1,0:T(8,128)(2,1)} async-done(((bf16[2048,768]{1,0:T(8,128)(2,1)}), bf16[512,768]{1,0:T(8,128)(2,1)}) %reduce-scatter.20.cloned.1.call-update) | async-done | bytes 786448 | tf_op jit(solution)/shard_map/reduce_scatter | solution.py:188
  231.1 26.3 %all-gather.2 = bf16[8,1,384]{2,1,0:T(2,128)(2,1)S(1)} all-gather(bf16[1,1,384]{2,1,0:T(2,128)(2,1)S(1)} %reshape.272), channel_id=1, replica_groups=mesh['dp'=8,'tensor'=4] {'dp'}, dimensions={0}, use_global_device_ids=true | all-gather | bytes 6912 | tf_op jit(solution)/shard_map/all_gather | solution.py:150
  259.5 19.0 %multiply_convert_fusion.1 = (bf16[2048,768]{1,0:T(8,128)(2,1)}, f32[2048,768]{1,0:T(8,128)}, f32[2048,768]{1,0:T(8,128)}) fusion(f32[768]{0:T(1024)S(1)} %dynamic_slice.75, bf16[2048,768]{1,0:T(8,128)(2,1)} %all-gather.11.cloned.1.call-done, bf16[768,768]{1,0:T(8,128)(2,1)} %all-gather.13.cloned.1.call-done), kind=kOutput, calls=%fused_computation.62 | convolution fusion | flops 2519728128 | bytes 20057088 | tf_op jit(solution)/shard_map/dot_general | solution.py:199
  278.5 25.1 %all-gather.15.cloned.1.call-done = bf16[768,768]{0,1:T(8,128)(2,1)} async-done(((bf16[768,96]{0,1:T(8,128)(2,1)}), bf16[768,768]{0,1:T(8,128)(2,1)}) %all-gather.15.cloned.1.call-update) | async-done | bytes 1179664 | tf_op jit(solution)/shard_map/all_gather | solution.py:146
  303.6 6.5 convolution_convert_fusion.1
  311.2 30.6 %all_gather.42 = bf16[768,128]{1,0:T(8,128)(2,1)S(1)} all-gather(bf16[96,128]{1,0:T(8,128)(2,1)S(1)} %convert_element_type.175), channel_id=1, replica_groups=mesh['dp'=8,'tensor'=4] {'dp'}, dimensions={0}, use_global_device_ids=true | all-gather | bytes 221184 | tf_op jit(solution)/shard_map/all_gather | solution.py:147
  354.0 9.5 collective-permute-done
  367.0 34.9 %collective-permute-done.1 = bf16[1024,768]{1,0:T(8,128)(2,1)} collective-permute-done((bf16[1024,768]{1,0:T(8,128)(2,1)}, bf16[1024,768]{1,0:T(8,128)(2,1)}, u32[]{:S(2)}, u32[]{:S(2)}) %collective-permute-start.1) | collective-permute-done | bytes 1572896 | tf_op jit(solution)/shard_map/ppermute | solution.py:232
  409.1 10.1 convert_reduce_fusion
  425.0 39.1 %reduce-scatter.24.cloned.1.call-done = bf16[512,768]{1,0:T(8,128)(2,1)} async-done(((bf16[2048,768]{1,0:T(8,128)(2,1)}), bf16[512,768]{1,0:T(8,128)(2,1)}) %reduce-scatter.24.cloned.1.call-update) | async-done | bytes 786448 | tf_op jit(solution)/shard_map/reduce_scatter | solution.py:247
  484.5 19.6 %all-gather.17.cloned.1.call-done = bf16[2048,768]{1,0:T(8,128)(2,1)} async-done(((bf16[512,768]{1,0:T(8,128)(2,1)}), bf16[2048,768]{1,0:T(8,128)(2,1)}) %all-gather.17.cloned.1.call-update) | async-done | bytes 3145744 | tf_op jit(solution)/shard_map/all_gather | solution.py:255
  514.2 119.8 %while.45 = (s32[]{:T(128)}, f32[2048,3,64]{0,2,1:T(8,128)S(1)}, f32[2048,3,64]{0,2,1:T(8,128)}, bf16[4,512,3,64]{1,3,2,0:T(8,128)(2,1)}, s32[4]{0:T(128)S(1)}, ...) while((s32[]{:T(128)}, f32[2048,3,64]{0,2,1:T(8,128)S(1)}, ...), condition=%wide.region_20.21_spmd.clone, body=%wide.region_18.20_spmd.clone.sunk | while | flops 2062516736 | bytes 129419512 | solution.py:111
  520.9 4.9 fusion.153
  525.8 4.8 multiply_reduce_fusion.10
  530.7 5.0 multiply_convert_fusion.3
  535.6 5.7 fusion.154
  550.3 5.5 fusion.153
  560.7 5.0 multiply_convert_fusion.3
  565.7 5.6 fusion.154
  580.4 5.5 fusion.153
  585.9 4.8 multiply_reduce_fusion.10
  590.7 5.0 multiply_convert_fusion.3
  595.7 5.7 fusion.154
  610.4 5.5 fusion.153
  620.8 5.0 multiply_convert_fusion.3
  625.8 5.6 fusion.154
  640.3 10.6 all-reduce.1
  669.2 13.4 %gather_fusion.2 = f32[2048,768]{1,0:T(8,128)} fusion(f32[2048,768]{1,0:T(8,128)} %get-tuple-element.574, s32[2048]{0:T(1024)S(1)} %broadcast_clamp_fusion), kind=kCustom, calls=%fused_computation.2 | custom fusion | bytes 12591104 | tf_op jit(solution)/shard_map/jit(_take)/gather | solution.py:283
  682.6 7.0 copy.72
  689.6 18.9 %gather_fusion.1 = bf16[2048,3,192]{2,1,0:T(4,128)(2,1)} fusion(bf16[3,2048,192]{2,0,1:T(4,128)(2,1)} %copy.72, s32[2048]{0:T(1024)S(1)} %broadcast_clamp_fusion), kind=kCustom, calls=%fused_computation.1 | custom fusion | bytes 4726784 | tf_op jit(solution)/shard_map/jit(_take)/gather | solution.py:280
  708.4 9.7 select_bitcast_fusion
  718.1 6.3 fusion.48
  726.5 6.9 fusion.89
  733.5 7.0 fusion.57
  742.7 37.3 %all-reduce = f32[3072]{0:T(1024)S(1)} all-reduce(bf16[3072]{0:T(1024)(128)(2,1)S(1)} %get-tuple-element.552), channel_id=13, replica_groups=mesh['dp'=8,'tensor'=4] {'dp'}, use_global_device_ids=true, to_apply=%region_41.42.clone | all-reduce | flops 3072 | bytes 18432
  783.5 62.3 %reduce-scatter.36.cloned.1.call-done = f32[96,192]{1,0:T(8,128)} async-done(((f32[768,192]{1,0:T(8,128)}), f32[96,192]{1,0:T(8,128)}) %reduce-scatter.36.cloned.1.call-update) | async-done | bytes 73744
  847.4 68.1 %reduce-scatter.34.cloned.1.call-done = f32[96,576]{1,0:T(8,128)} async-done(((f32[768,576]{1,0:T(8,128)}), f32[96,576]{1,0:T(8,128)}) %reduce-scatter.34.cloned.1.call-update) | async-done | bytes 221200
  917.3 37.3 %reduce-scatter.26.cloned.1.call-done = bf16[512,768]{1,0:T(8,128)(2,1)} async-done(((bf16[2048,768]{1,0:T(8,128)(2,1)}), bf16[512,768]{1,0:T(8,128)(2,1)}) %reduce-scatter.26.cloned.1.call-update) | async-done | bytes 786448 | tf_op jit(solution)/shard_map/reduce_scatter | solution.py:282
  957.0 63.5 %reduce-scatter.32.cloned.1.call-done = f32[96,128]{1,0:T(8,128)} async-done(((f32[768,128]{1,0:T(8,128)}), f32[96,128]{1,0:T(8,128)}) %reduce-scatter.32.cloned.1.call-update) | async-done | bytes 49168 | tf_op jit(solution)/shard_map/reduce_scatter | solution.py:311
  1020.5 73.3 %reduce-scatter.28.cloned.1.call-done = f32[96,768]{1,0:T(8,128)} async-done(((f32[768,768]{1,0:T(8,128)}), f32[96,768]{1,0:T(8,128)}) %reduce-scatter.28.cloned.1.call-update) | async-done | bytes 294928 | tf_op jit(solution)/shard_map/reduce_scatter | solution.py:309
  1093.8 72.9 %reduce-scatter.30.cloned.1.call-done = f32[768,96]{0,1:T(8,128)} async-done(((f32[768,768]{0,1:T(8,128)}), f32[768,96]{0,1:T(8,128)}) %reduce-scatter.30.cloned.1.call-update) | async-done | bytes 294928 | tf_op jit(solution)/shard_map/reduce_scatter | solution.py:310
  (302 shorter events, 201.3 us)
Async XLA Ops:
  8.0 68.9 %copy-start.21 = (s32[1,2048]{1,0:T(1,128)S(1)}, s32[1,2048]{1,0:T(1,128)}, u32[]{:S(2)}) copy-start(s32[1,2048]{1,0:T(1,128)} %param.18) | copy-start | bytes 24580
  8.0 109.0 %all-gather.9.cloned.1.call-start = ((), (), s32[]{:S(2)}) async-start(), calls=%async_computation.11 | async-start | bytes 3932160 | tf_op jit(solution)/shard_map/all_gather | solution.py:164
  8.8 215.3 %reduce-scatter.20.cloned.1.call-start = ((), (), s32[]{:S(2)}) async-start(), calls=%async_computation.12 | async-start | bytes 3932160 | tf_op jit(solution)/shard_map/reduce_scatter | solution.py:188
  76.8 54.8 %copy-start.14 = (bf16[3,768,192]{1,2,0:T(8,128)(2,1)}, bf16[3,768,192]{1,2,0:T(8,128)(2,1)S(1)}, u32[]{:S(2)}) copy-start(bf16[3,768,192]{1,2,0:T(8,128)(2,1)S(1)} %copy.62) | copy-start | bytes 2654212
  76.9 52.5 %copy-start.23 = (s32[2048,1]{0,1:T(1,128)}, s32[2048,1]{0,1:T(1,128)S(1)}, u32[]{:S(2)}) copy-start(s32[2048,1]{0,1:T(1,128)S(1)} %compare_select_fusion) | copy-start | bytes 24580
  185.1 4.5 copy-start.42
  187.9 69.6 %all-gather.13.cloned.1.call-start = ((), (), s32[]{:S(2)}) async-start(), calls=%async_computation.14 | async-start | bytes 1327104 | tf_op jit(solution)/shard_map/all_gather | solution.py:145
  189.6 69.9 %all-gather.11.cloned.1.call-start = ((), (), s32[]{:S(2)}) async-start(), calls=%async_computation.13 | async-start | bytes 3932160 | tf_op jit(solution)/shard_map/all_gather | solution.py:197
  224.1 6.2 copy-start.17
  224.1 7.0 copy-start.39
  230.2 73.3 %all-gather.15.cloned.1.call-start = ((), (), s32[]{:S(2)}) async-start(), calls=%async_computation.15 | async-start | bytes 1327104 | tf_op jit(solution)/shard_map/all_gather | solution.py:146
  231.0 115.3 %reduce-scatter.22.cloned.1.call-start = ((), (), s32[]{:S(2)}) async-start(), calls=%async_computation.16 | async-start | bytes 3932160 | tf_op jit(solution)/shard_map/reduce_scatter | solution.py:201
  257.5 21.0 %copy-start.37 = (f32[768]{0:T(1024)}, f32[768]{0:T(1024)S(1)}, u32[]{:S(2)}) copy-start(f32[768]{0:T(1024)S(1)} %dynamic_slice.75) | copy-start | bytes 9220
  310.1 36.2 %copy-start.20 = (f32[768]{0:T(1024)S(1)}, f32[768]{0:T(1024)}, u32[]{:S(2)}) copy-start(f32[768]{0:T(1024)} %get-tuple-element.508) | copy-start | bytes 9220
  310.1 36.2 %copy-start.30 = (f32[768]{0:T(1024)S(1)}, f32[768]{0:T(1024)}, u32[]{:S(2)}) copy-start(f32[768]{0:T(1024)} %get-tuple-element.507) | copy-start | bytes 9220
  310.1 38.7 %copy-start.29 = (f32[768]{0:T(1024)S(1)}, f32[768]{0:T(1024)}, u32[]{:S(2)}) copy-start(f32[768]{0:T(1024)} %get-tuple-element.506) | copy-start | bytes 9220
  310.2 153.9 %reduce-scatter.24.cloned.1.call-start = ((), (), s32[]{:S(2)}) async-start(), calls=%async_computation.17 | async-start | bytes 3932160 | tf_op jit(solution)/shard_map/reduce_scatter | solution.py:247
  352.4 12.4 %copy-start.2 = (f32[512,768]{1,0:T(8,128)}, f32[512,768]{1,0:T(8,128)S(1)}, u32[]{:S(2)}) copy-start(f32[512,768]{1,0:T(8,128)S(1)} %get-tuple-element.560) | copy-start | bytes 4718596
  352.4 12.4 %copy-start.25 = (f32[512]{0:T(512)}, f32[512]{0:T(512)S(1)}, u32[]{:S(2)}) copy-start(f32[512]{0:T(512)S(1)} %negate_multiply_fusion.2) | copy-start | bytes 6148
  353.6 9.9 copy-start.7
  353.7 9.9 collective-permute-start
  364.8 37.1 %collective-permute-start.1 = (bf16[1024,768]{1,0:T(8,128)(2,1)}, bf16[1024,768]{1,0:T(8,128)(2,1)}, u32[]{:S(2)}, u32[]{:S(2)}) collective-permute-start(bf16[1024,768]{1,0:T(8,128)(2,1)} %pad_maximum_fusion.1), channel_id=1, source_target_pairs={{0,2},{1,3},{2,0},{3,1},{4,6},{5,7},{6,4},{7,5},{8,10},{9,11},{10,... | collective-permute-start | bytes 4718600 | tf_op jit(solution)/shard_map/ppermute | solution.py:232
  366.0 38.5 %copy-start.8 = (bf16[512,768]{1,0:T(8,128)(2,1)S(1)}, bf16[512,768]{1,0:T(8,128)(2,1)}, u32[]{:S(2)}) copy-start(bf16[512,768]{1,0:T(8,128)(2,1)} %copy-done.7) | copy-start | bytes 2359300
  404.5 4.6 copy-start.38
  404.5 4.6 copy-start.41
  409.1 11.8 %copy-start.40 = (bf16[768,768]{1,0:T(8,128)(2,1)S(1)}, bf16[768,768]{1,0:T(8,128)(2,1)}, u32[]{:S(2)}) copy-start(bf16[768,768]{1,0:T(8,128)(2,1)} %all-gather.13.cloned.1.call-done) | copy-start | bytes 3538948
  424.9 79.2 %all-gather.17.cloned.1.call-start = ((), (), s32[]{:S(2)}) async-start(), calls=%async_computation.18 | async-start | bytes 3932160 | tf_op jit(solution)/shard_map/all_gather | solution.py:255
  464.1 4.3 copy-start.11
  475.3 249.1 %all-reduce.4.cloned.1.call-start = ((), (), s32[]{:S(2)}) async-start(), calls=%async_computation.22 | async-start | bytes 393216 | tf_op jit(solution)/shard_map/psum | solution.py:301
  478.9 301.6 %reduce-scatter.38.cloned.1.call-start = ((), (), s32[]{:S(2)}) async-start(), calls=%async_computation.26 | async-start | bytes 442368
  480.1 33.2 %copy-start.26 = (bf16[3072]{0:T(1024)(128)(2,1)}, bf16[3072]{0:T(1024)(128)(2,1)S(1)}, u32[]{:S(2)}) copy-start(bf16[3072]{0:T(1024)(128)(2,1)S(1)} %dynamic_update_slice.46) | copy-start | bytes 18436
  535.6 5.7 copy-start
  565.7 5.6 copy-start
  595.7 5.7 copy-start
  625.8 5.6 copy-start
  638.0 14.9 %copy-start.10 = (bf16[24,8,4,512]{3,1,2,0:T(8,128)(2,1)S(1)}, bf16[24,8,4,512]{3,1,2,0:T(8,128)(2,1)}, u32[]{:S(2)}) copy-start(bf16[24,8,4,512]{3,1,2,0:T(8,128)(2,1)} %copy-done.9) | copy-start | bytes 2359300
  651.8 130.2 %reduce-scatter.40.cloned.1.call-start = ((), (), s32[]{:S(2)}) async-start(), calls=%async_computation.27 | async-start | bytes 442368
  652.8 192.9 %reduce-scatter.36.cloned.1.call-start = ((), (), s32[]{:S(2)}) async-start(), calls=%async_computation.25 | async-start | bytes 884736
  657.0 258.5 %reduce-scatter.34.cloned.1.call-start = ((), (), s32[]{:S(2)}) async-start(), calls=%async_computation.24 | async-start | bytes 2211840
  664.4 4.8 copy-start.22
  664.4 4.8 copy-start.24
  669.1 285.5 %reduce-scatter.26.cloned.1.call-start = ((), (), s32[]{:S(2)}) async-start(), calls=%async_computation.19 | async-start | bytes 3932160 | tf_op jit(solution)/shard_map/reduce_scatter | solution.py:282
  708.4 9.7 copy-start.15
  724.4 296.1 %reduce-scatter.32.cloned.1.call-start = ((), (), s32[]{:S(2)}) async-start(), calls=%async_computation.23 | async-start | bytes 442368 | tf_op jit(solution)/shard_map/reduce_scatter | solution.py:311
  726.2 367.6 %reduce-scatter.28.cloned.1.call-start = ((), (), s32[]{:S(2)}) async-start(), calls=%async_computation.20 | async-start | bytes 2654208 | tf_op jit(solution)/shard_map/reduce_scatter | solution.py:309
  733.5 7.1 copy-start.43
  733.5 8.3 copy-start.13
  733.5 433.3 %reduce-scatter.30.cloned.1.call-start = ((), (), s32[]{:S(2)}) async-start(), calls=%async_computation.21 | async-start | bytes 2654208 | tf_op jit(solution)/shard_map/reduce_scatter | solution.py:310
  (19 other events, 53.6 us)
Sparse Core Ops, SparseCore 0:
  10.4 31.2 all-gather.8
  188.0 35.9 reduce-scatter.19
  425.1 38.9 reduce-scatter.23
  479.1 47.6 all-reduce.3
Sparse Core Ops, SparseCore 1:
  191.2 39.5 all-gather.12
  232.7 26.7 all-gather.10
  262.1 41.4 all-gather.14
  310.2 36.1 reduce-scatter.21
  475.4 28.6 all-gather.16
  651.9 63.3 reduce-scatter.37
  718.4 61.1 reduce-scatter.39
  783.4 62.3 reduce-scatter.35
  849.1 66.3 reduce-scatter.33
  918.0 36.6 reduce-scatter.25
  958.3 62.2 reduce-scatter.31
  1024.6 69.1 reduce-scatter.27
  1097.8 68.9 reduce-scatter.29
